TPU v7x, 32 devices: a whole 2x2x4 slice. The times are simulated.
32 devices in a mesh: dp: 8 (over z, x), mp: 4 (over y, core).
Axes of the slice: x: 2, y: 2, z: 4, core: 2. Of those that a mesh axis runs over, the one named last changes fastest.
Arguments:
- text_blocks: bfloat16 [256, 64, 768], P(('dp', 'mp')), may hold values from -6 to 6
- visual_blocks: bfloat16 [256, 40, 768], P(('dp', 'mp')), may hold values from -6 to 6
- drop_flags: int32 [256, 2], P('dp'), may hold values 0 or 1
- qkv_weight: bfloat16 [4, 768, 3, 768], P(None, None, None, 'mp'), may hold values from -0.21875 to 0.21875
- out_weight: bfloat16 [4, 768, 768], P(None, 'mp'), may hold values from -0.625 to 0.625
- up_weight: bfloat16 [2, 768, 3072], P(None, None, 'mp'), may hold values from -0.21875 to 0.21875
- down_weight: bfloat16 [2, 3072, 768], P(None, 'mp'), may hold values from -0.109375 to 0.109375
- norm_gain: float32 [6, 768], replicated, may hold values from 0.5 to 1.5
- norm_shift: float32 [6, 768], replicated, may hold values from -3 to 3
- text_cotangent: bfloat16 [256, 64, 768], P(('dp', 'mp')), may hold values from -6 to 6
- visual_cotangent: bfloat16 [256, 40, 768], P(('dp', 'mp')), may hold values from -6 to 6
Outputs:
- text_output: bfloat16 [256, 64, 768], P(('dp', 'mp'))
- visual_output: bfloat16 [256, 40, 768], P(('dp', 'mp'))
- text_gradient: bfloat16 [256, 64, 768], P(('dp', 'mp'))
- visual_gradient: bfloat16 [256, 40, 768], P(('dp', 'mp'))
- qkv_gradient: float32 [4, 768, 3, 768], P(None, None, None, 'mp')
- out_gradient: float32 [4, 768, 768], P(None, 'mp')
- up_gradient: float32 [2, 768, 3072], P(None, None, 'mp')
- down_gradient: float32 [2, 3072, 768], P(None, 'mp')
- gain_gradient: float32 [6, 768], replicated
- shift_gradient: float32 [6, 768], replicated
Inputs may be any that keep to these rules, and one draw needn't show every extreme that they name: drop_flags[:, 0] = 1 marks a page whose text is absent, drop_flags[:, 1] = 1 one whose visual blocks are absent.
All inputs are finite; a program needn't handle non-finite values.
Results may differ from a plain program's by a relative error of at most 0.025.
Values may be sent and summed in bfloat16 or wider, within the bound.
No kernel may reach another device: no remote copies, remote signals or barrier semaphores. Data moves between devices by JAX's collectives and lax.ppermute only.
A program may use at most 256 MiB of HBM per device.

v0:
```python
import jax
import jax.numpy as jnp
from jax import lax
from jax.sharding import PartitionSpec as P

HEAD = 64
EPSILON = 1e-05


def normalize(values, gain, shift):
    center = values - jnp.mean(values, axis=-1, keepdims=True)
    spread = jnp.mean(center * center, axis=-1, keepdims=True)
    return center * lax.rsqrt(spread + EPSILON) * gain + shift


def linear(activation, weight):
    return jnp.einsum("pld,de->ple", activation, weight, preferred_element_type=jnp.float32)


def linear_back(gradient, weight):
    return jnp.einsum("ple,de->pld", gradient, weight, preferred_element_type=jnp.float32)


def weight_grad(activation, gradient):
    return jnp.einsum("pld,ple->de", activation, gradient, preferred_element_type=jnp.float32)


def split_heads(values):
    return values.reshape(values.shape[0], values.shape[1], values.shape[2] // HEAD, HEAD)


def merge_heads(values):
    return values.reshape(values.shape[0], values.shape[1], values.shape[2] * values.shape[3])


def score_block(queries, key_block):
    raw = jnp.einsum(
        "pqhe,pkhe->phqk",
        split_heads(queries),
        split_heads(key_block),
        preferred_element_type=jnp.float32,
    )
    return raw * HEAD ** (-0.5)


def attend_context(query_side, key_side, weight_block, keep_mask):
    queries = linear(query_side, weight_block[:, 0]).astype(jnp.bfloat16)
    key_block = linear(key_side, weight_block[:, 1]).astype(jnp.bfloat16)
    value_block = linear(key_side, weight_block[:, 2]).astype(jnp.bfloat16)
    scores = score_block(queries, key_block)
    row_max = jnp.max(scores, axis=-1, keepdims=True)
    log_total = row_max + jnp.log(jnp.sum(jnp.exp(scores - row_max), axis=-1, keepdims=True))
    probability = jnp.exp(scores - log_total).astype(jnp.bfloat16)
    context = merge_heads(
        jnp.einsum(
            "phqk,pkhe->pqhe",
            probability,
            split_heads(value_block),
            preferred_element_type=jnp.float32,
        )
    )
    if keep_mask is not None:
        context = context * keep_mask[:, None, None]
    context = context.astype(jnp.bfloat16)
    return (context, (queries, key_block, value_block, log_total, context))


def attend_back(query_side, key_side, weight_block, out_block, keep_mask, saved, out_grad):
    queries, key_block, value_block, log_total, context = saved
    out_weight_grad = weight_grad(context, out_grad)
    context_grad = linear_back(out_grad, out_block).astype(jnp.bfloat16)
    if keep_mask is not None:
        context_grad = context_grad * keep_mask[:, None, None].astype(jnp.bfloat16)
    probability = jnp.exp(score_block(queries, key_block) - log_total)
    heads_grad = split_heads(context_grad)
    prob_grad = jnp.einsum(
        "pqhe,pkhe->phqk", heads_grad, split_heads(value_block), preferred_element_type=jnp.float32
    )
    value_grad = merge_heads(
        jnp.einsum(
            "phqk,pqhe->pkhe",
            probability.astype(jnp.bfloat16),
            heads_grad,
            preferred_element_type=jnp.float32,
        )
    ).astype(jnp.bfloat16)
    score_grad = (
        probability * (prob_grad - jnp.sum(prob_grad * probability, axis=-1, keepdims=True))
    ).astype(jnp.bfloat16)
    query_grad = (
        merge_heads(
            jnp.einsum(
                "phqk,pkhe->pqhe",
                score_grad,
                split_heads(key_block),
                preferred_element_type=jnp.float32,
            )
        )
        * HEAD ** (-0.5)
    ).astype(jnp.bfloat16)
    key_grad = (
        merge_heads(
            jnp.einsum(
                "phqk,pqhe->pkhe",
                score_grad,
                split_heads(queries),
                preferred_element_type=jnp.float32,
            )
        )
        * HEAD ** (-0.5)
    ).astype(jnp.bfloat16)
    in_weight_grad = jnp.stack(
        [
            weight_grad(query_side, query_grad),
            weight_grad(key_side, key_grad),
            weight_grad(key_side, value_grad),
        ],
        axis=1,
    )
    query_back = linear_back(query_grad, weight_block[:, 0])
    key_back = linear_back(key_grad, weight_block[:, 1]) + linear_back(
        value_grad, weight_block[:, 2]
    )
    return (in_weight_grad, out_weight_grad, query_back, key_back)


def feed_forward(activation, up_block, down_block):
    before = linear(activation, up_block)
    hidden = jax.nn.gelu(before).astype(jnp.bfloat16)
    return (linear(hidden, down_block), (before, hidden))


def feed_back(activation, up_block, down_block, saved, out_grad):
    before, hidden = saved
    down_grad = weight_grad(hidden, out_grad)
    hidden_grad = linear_back(out_grad, down_block)
    gelu_pull = jax.vjp(jax.nn.gelu, before)[1]
    before_grad = gelu_pull(hidden_grad)[0].astype(jnp.bfloat16)
    up_grad = weight_grad(activation, before_grad)
    return (up_grad, down_grad, linear_back(before_grad, up_block))


def per_device(
    text_blocks,
    visual_blocks,
    drop_flags,
    qkv_weight,
    out_weight,
    up_weight,
    down_weight,
    norm_gain,
    norm_shift,
    text_cotangent,
    visual_cotangent,
):
    keep_text = (1 - drop_flags[:, 0]).astype(jnp.float32)
    keep_visual = (1 - drop_flags[:, 1]).astype(jnp.float32)
    text_now = text_blocks.astype(jnp.float32)
    visual_now = visual_blocks.astype(jnp.float32)
    inputs = []
    gathered = []
    saved = []
    for sublayer in range(3):
        inputs.append((text_now, visual_now))
        text_norm = normalize(text_now, norm_gain[2 * sublayer], norm_shift[2 * sublayer]).astype(
            jnp.bfloat16
        )
        visual_norm = normalize(
            visual_now, norm_gain[2 * sublayer + 1], norm_shift[2 * sublayer + 1]
        ).astype(jnp.bfloat16)
        text_rows, visual_rows = (
            lax.all_gather(text_norm, "mp", axis=0, tiled=True),
            lax.all_gather(visual_norm, "mp", axis=0, tiled=True),
        )
        gathered.append((text_rows, visual_rows))
        text_part = None
        visual_part = None
        if sublayer < 2:
            if sublayer == 0:
                text_context, text_saved = attend_context(
                    text_rows, visual_rows, qkv_weight[0], keep_visual
                )
                visual_context, visual_saved = attend_context(
                    visual_rows, text_rows, qkv_weight[1], keep_text
                )
            else:
                text_context, text_saved = attend_context(text_rows, text_rows, qkv_weight[2], None)
                visual_context, visual_saved = attend_context(
                    visual_rows, visual_rows, qkv_weight[3], None
                )
            text_part = linear(text_context, out_weight[2 * sublayer])
            visual_part = linear(visual_context, out_weight[2 * sublayer + 1])
        else:
            text_part, text_saved = feed_forward(text_rows, up_weight[0], down_weight[0])
            visual_part, visual_saved = feed_forward(visual_rows, up_weight[1], down_weight[1])
        text_added, visual_added = (
            lax.psum_scatter(
                text_part.astype(jnp.bfloat16), "mp", scatter_dimension=0, tiled=True
            ).astype(jnp.float32),
            lax.psum_scatter(
                visual_part.astype(jnp.bfloat16), "mp", scatter_dimension=0, tiled=True
            ).astype(jnp.float32),
        )
        saved.append((text_saved, visual_saved))
        text_now = text_now + text_added
        visual_now = visual_now + visual_added
    text_output = text_now.astype(jnp.bfloat16)
    visual_output = visual_now.astype(jnp.bfloat16)
    text_back = text_cotangent.astype(jnp.float32)
    visual_back = visual_cotangent.astype(jnp.float32)
    in_parts = [None, None, None, None]
    out_parts = [None, None, None, None]
    gain_parts = [None, None, None, None, None, None]
    shift_parts = [None, None, None, None, None, None]
    up_grads = None
    down_grads = None
    for sublayer in (2, 1, 0):
        text_branch, visual_branch = (
            lax.all_gather(text_back.astype(jnp.bfloat16), "mp", axis=0, tiled=True),
            lax.all_gather(visual_back.astype(jnp.bfloat16), "mp", axis=0, tiled=True),
        )
        text_rows, visual_rows = gathered[sublayer]
        text_saved, visual_saved = saved[sublayer]
        if sublayer == 2:
            up_text, down_text, text_part = feed_back(
                text_rows, up_weight[0], down_weight[0], text_saved, text_branch
            )
            up_visual, down_visual, visual_part = feed_back(
                visual_rows, up_weight[1], down_weight[1], visual_saved, visual_branch
            )
            up_grads = jnp.stack([up_text, up_visual])
            down_grads = jnp.stack([down_text, down_visual])
        elif sublayer == 1:
            in_parts[2], out_parts[2], query_back, key_back = attend_back(
                text_rows, text_rows, qkv_weight[2], out_weight[2], None, text_saved, text_branch
            )
            text_part = query_back + key_back
            in_parts[3], out_parts[3], query_back, key_back = attend_back(
                visual_rows,
                visual_rows,
                qkv_weight[3],
                out_weight[3],
                None,
                visual_saved,
                visual_branch,
            )
            visual_part = query_back + key_back
        else:
            in_parts[0], out_parts[0], text_query_back, visual_key_back = attend_back(
                text_rows,
                visual_rows,
                qkv_weight[0],
                out_weight[0],
                keep_visual,
                text_saved,
                text_branch,
            )
            in_parts[1], out_parts[1], visual_query_back, text_key_back = attend_back(
                visual_rows,
                text_rows,
                qkv_weight[1],
                out_weight[1],
                keep_text,
                visual_saved,
                visual_branch,
            )
            text_part = text_query_back + text_key_back
            visual_part = visual_query_back + visual_key_back
        text_norm_grad, visual_norm_grad = (
            lax.psum_scatter(
                text_part.astype(jnp.bfloat16), "mp", scatter_dimension=0, tiled=True
            ).astype(jnp.float32),
            lax.psum_scatter(
                visual_part.astype(jnp.bfloat16), "mp", scatter_dimension=0, tiled=True
            ).astype(jnp.float32),
        )
        text_in, visual_in = inputs[sublayer]
        text_pull = jax.vjp(normalize, text_in, norm_gain[2 * sublayer], norm_shift[2 * sublayer])[
            1
        ]
        text_delta, gain_parts[2 * sublayer], shift_parts[2 * sublayer] = text_pull(text_norm_grad)
        visual_pull = jax.vjp(
            normalize, visual_in, norm_gain[2 * sublayer + 1], norm_shift[2 * sublayer + 1]
        )[1]
        visual_delta, gain_parts[2 * sublayer + 1], shift_parts[2 * sublayer + 1] = visual_pull(
            visual_norm_grad
        )
        text_back = text_back + text_delta
        visual_back = visual_back + visual_delta
    gain_grads = jnp.stack(gain_parts)
    shift_grads = jnp.stack(shift_parts)
    gain_grads, shift_grads = (
        lax.psum(gain_grads.astype(jnp.bfloat16), "mp").astype(jnp.float32),
        lax.psum(shift_grads.astype(jnp.bfloat16), "mp").astype(jnp.float32),
    )
    in_grads = jnp.stack(in_parts)
    out_grads = jnp.stack(out_parts)
    in_grads, out_grads, up_grads, down_grads = jax.tree.map(
        lambda grad: lax.psum(grad.astype(jnp.bfloat16), "dp").astype(jnp.float32),
        (in_grads, out_grads, up_grads, down_grads),
    )
    gain_grads, shift_grads = lax.psum((gain_grads, shift_grads), "dp")
    return (
        text_output,
        visual_output,
        text_back.astype(jnp.bfloat16),
        visual_back.astype(jnp.bfloat16),
        in_grads,
        out_grads,
        up_grads,
        down_grads,
        gain_grads,
        shift_grads,
    )


def solution(mesh):
    placed = (
        P(("dp", "mp"), None, None),
        P(("dp", "mp"), None, None),
        P("dp", None),
        P(None, None, None, "mp"),
        P(None, "mp", None),
        P(None, None, "mp"),
        P(None, "mp", None),
        P(),
        P(),
        P(("dp", "mp"), None, None),
        P(("dp", "mp"), None, None),
    )
    return jax.shard_map(
        per_device,
        mesh=mesh,
        in_specs=placed,
        out_specs=(
            P(("dp", "mp"), None, None),
            P(("dp", "mp"), None, None),
            P(("dp", "mp"), None, None),
            P(("dp", "mp"), None, None),
            P(None, None, None, "mp"),
            P(None, "mp", None),
            P(None, None, "mp"),
            P(None, "mp", None),
            P(),
            P(),
        ),
        check_vma=False,
    )
```

profile of v0, /device:TPU:0, one launch (start us, length us, event | category | flops | bytes accessed | tf_op | source)
XLA Modules:
  0.0 1164.1 jit_solution(13793235685979987641)
XLA Ops:
  20.7 18.6 %all-gather.13.cloned.1.call-done = bf16[32,40,768]{2,1,0:T(8,128)(2,1)} async-done(((bf16[8,40,768]{2,1,0:T(8,128)(2,1)}), bf16[32,40,768]{2,1,0:T(8,128)(2,1)}) %all-gather.13.cloned.1.call-update) | async-done | bytes 1966096 | tf_op jit(solution)/shard_map/all_gather | solution.py:173
  42.8 27.1 %all-gather.15.cloned.1.call-done = bf16[32,64,768]{2,1,0:T(8,128)(2,1)} async-done(((bf16[8,64,768]{2,1,0:T(8,128)(2,1)}), bf16[32,64,768]{2,1,0:T(8,128)(2,1)}) %all-gather.15.cloned.1.call-update) | async-done | bytes 3145744 | tf_op jit(solution)/shard_map/all_gather | solution.py:172
  69.9 3.9 convolution_convert_fusion.13
  75.6 4.4 convolution_convert_fusion.14
  100.8 4.1 convolution_convert_fusion.18
  114.1 3.9 convolution_convert_fusion.3
  118.0 5.9 reduce-scatter.19.cloned.1.call-done
  127.7 37.1 %reduce-scatter.13.cloned.1.call-done = bf16[8,64,768]{2,1,0:T(8,128)(2,1)} async-done(((bf16[32,64,768]{2,1,0:T(8,128)(2,1)}), bf16[8,64,768]{2,1,0:T(8,128)(2,1)}) %reduce-scatter.13.cloned.1.call-update) | async-done | bytes 786448 | tf_op jit(solution)/shard_map/reduce_scatter | solution.py:197
  168.6 20.0 %all-gather.21.cloned.1.call-done = bf16[32,40,768]{2,1,0:T(8,128)(2,1)} async-done(((bf16[8,40,768]{2,1,0:T(8,128)(2,1)}), bf16[32,40,768]{2,1,0:T(8,128)(2,1)}) %all-gather.21.cloned.1.call-update) | async-done | bytes 1966096 | tf_op jit(solution)/shard_map/all_gather | solution.py:173
  198.0 3.9 convolution_convert_fusion.26
  201.9 3.6 reshape.435
  219.2 3.9 convolution_convert_fusion.15
  225.6 3.9 convolution_convert_fusion.16
  232.0 3.9 convolution_convert_fusion.17
  244.0 3.9 convolution_convert_fusion.2
  248.0 4.7 reduce-scatter.21.cloned.1.call-done
  256.6 37.1 %reduce-scatter.15.cloned.1.call-done = bf16[8,64,768]{2,1,0:T(8,128)(2,1)} async-done(((bf16[32,64,768]{2,1,0:T(8,128)(2,1)}), bf16[8,64,768]{2,1,0:T(8,128)(2,1)}) %reduce-scatter.15.cloned.1.call-update) | async-done | bytes 786448 | tf_op jit(solution)/shard_map/reduce_scatter | solution.py:197
  297.9 19.9 %all-gather.23.cloned.1.call-done = bf16[32,40,768]{2,1,0:T(8,128)(2,1)} async-done(((bf16[8,40,768]{2,1,0:T(8,128)(2,1)}), bf16[32,40,768]{2,1,0:T(8,128)(2,1)}) %all-gather.23.cloned.1.call-update) | async-done | bytes 1966096 | tf_op jit(solution)/shard_map/all_gather | solution.py:173
  317.7 5.5 fusion.80
  323.2 17.8 %all-gather.31.cloned.1.call-done = bf16[32,40,768]{2,1,0:T(8,128)(2,1)} async-done(((bf16[8,40,768]{2,1,0:T(8,128)(2,1)}), bf16[32,40,768]{2,1,0:T(8,128)(2,1)}) %all-gather.31.cloned.1.call-update) | async-done | bytes 1966096 | tf_op jit(solution)/shard_map/all_gather | solution.py:220
  341.0 7.0 fusion.13
  352.7 18.9 %all-gather.19.cloned.1.call-done = bf16[32,64,768]{2,1,0:T(8,128)(2,1)} async-done(((bf16[8,64,768]{2,1,0:T(8,128)(2,1)}), bf16[32,64,768]{2,1,0:T(8,128)(2,1)}) %all-gather.19.cloned.1.call-update) | async-done | bytes 3145744 | tf_op jit(solution)/shard_map/all_gather | solution.py:172
  371.7 7.5 fusion.85
  379.2 22.4 %all-gather.25.cloned.1.call-done = bf16[32,64,768]{2,1,0:T(8,128)(2,1)} async-done(((bf16[8,64,768]{2,1,0:T(8,128)(2,1)}), bf16[32,64,768]{2,1,0:T(8,128)(2,1)}) %all-gather.25.cloned.1.call-update) | async-done | bytes 3145744 | tf_op jit(solution)/shard_map/all_gather | solution.py:219
  401.7 8.5 fusion.6
  411.8 4.1 convolution_convert_fusion
  415.9 18.7 %reduce-scatter.29.cloned.1.call-done = bf16[8,40,768]{2,1,0:T(8,128)(2,1)} async-done(((bf16[32,40,768]{2,1,0:T(8,128)(2,1)}), bf16[8,40,768]{2,1,0:T(8,128)(2,1)}) %reduce-scatter.29.cloned.1.call-update) | async-done | bytes 491536 | tf_op jit(solution)/shard_map/reduce_scatter | solution.py:273
  439.9 35.0 %reduce-scatter.25.cloned.1.call-done = bf16[8,64,768]{2,1,0:T(8,128)(2,1)} async-done(((bf16[32,64,768]{2,1,0:T(8,128)(2,1)}), bf16[8,64,768]{2,1,0:T(8,128)(2,1)}) %reduce-scatter.25.cloned.1.call-update) | async-done | bytes 786448 | tf_op jit(solution)/shard_map/reduce_scatter | solution.py:270
  479.8 18.9 %all-gather.33.cloned.1.call-done = bf16[32,40,768]{2,1,0:T(8,128)(2,1)} async-done(((bf16[8,40,768]{2,1,0:T(8,128)(2,1)}), bf16[32,40,768]{2,1,0:T(8,128)(2,1)}) %all-gather.33.cloned.1.call-update) | async-done | bytes 1966096 | tf_op jit(solution)/shard_map/all_gather | solution.py:220
  501.9 3.5 reshape.440
  505.4 3.8 multiply_reduce_fusion.3
  513.1 3.5 convert_element_type.540
  520.5 3.5 convert_element_type.543
  528.3 3.5 convert_element_type.546
  537.0 6.3 convolution_convert_fusion.5
  543.6 4.3 convolution_convert_fusion.12
  550.5 4.2 multiply_reduce_fusion
  561.6 4.0 fusion.36
  578.4 8.7 convolution_convert_fusion.1
  590.3 10.0 reduce-scatter.23.cloned.1.call-done
  600.3 3.9 fusion.209
  604.2 3.8 copy.219
  608.0 4.5 reshape.443
  612.5 3.6 copy.218
  616.1 24.6 %reduce-scatter.27.cloned.1.call-done = bf16[8,64,768]{2,1,0:T(8,128)(2,1)} async-done(((bf16[32,64,768]{2,1,0:T(8,128)(2,1)}), bf16[8,64,768]{2,1,0:T(8,128)(2,1)}) %reduce-scatter.27.cloned.1.call-update) | async-done | bytes 786448 | tf_op jit(solution)/shard_map/reduce_scatter | solution.py:270
  643.9 37.2 %reduce-scatter.17.cloned.1.call-done = bf16[8,64,768]{2,1,0:T(8,128)(2,1)} async-done(((bf16[32,64,768]{2,1,0:T(8,128)(2,1)}), bf16[8,64,768]{2,1,0:T(8,128)(2,1)}) %reduce-scatter.17.cloned.1.call-update) | async-done | bytes 786448 | tf_op jit(solution)/shard_map/reduce_scatter | solution.py:197
  681.0 4.1 fusion.210
  685.4 5.1 fusion.44
  699.5 5.5 all-gather.35.cloned.1.call-done
  708.3 3.7 reshape.441
  723.0 3.8 fusion.171
  726.7 9.0 all-gather.29.cloned.1.call-done
  735.7 3.9 fusion.49
  751.6 3.5 convert_element_type.567
  757.9 3.5 convert_element_type.570
  769.6 8.5 fusion.45
  782.5 3.9 convolution_convert_fusion.8
  786.4 5.1 fusion.172
  799.2 4.1 add_convert_fusion
  803.6 5.7 fusion.43
  849.5 10.7 all-reduce.2
  860.2 40.7 %all-reduce = (f32[6,768]{1,0:T(8,128)}, f32[6,768]{1,0:T(8,128)}) all-reduce(bf16[6,768]{1,0:T(8,128)(2,1)S(1)} %get-tuple-element.40, bf16[6,768]{1,0:T(8,128)(2,1)S(1)} %get-tuple-element.41), channel_id=1, replica_groups=mesh['dp'=8,'mp'=4] {'dp'}, use_global_device_ids=true, to_apply=%region_59.0 | all-reduce | flops 9216 | bytes 55296 | tf_op jit(solution)/shard_map/psum | solution.py:302
  903.9 241.7 %all-reduce.5.cloned.1.call-done = (bf16[4,768,3,192]{1,3,2,0:T(8,128)(2,1)}, bf16[4,192,768]{2,1,0:T(8,128)(2,1)}, bf16[2,768,768]{2,1,0:T(8,128)(2,1)}, bf16[2,768,768]{2,1,0:T(8,128)(2,1)}) async-done(((bf16[4,768,3,192]{1,3,2,0:T(8,128)(2,1)}, bf16[4,192,768]{2,1,0:T(8,128)(2,1)}, bf16[2,768,768]{2,1,0:T(8,128)(2,1)}, bf16[2,768,768]{2,1,0:T(8,128)(2,1)}), (bf16[4,768,3,192]{1,3,2,0:T(8,128)(2,1)}, ...) | async-done | bytes 9437200 | tf_op jit(solution)/shard_map/psum | solution.py:299
  1148.6 3.7 convert_element_type.574
  (508 shorter events, 275.0 us)
Async XLA Ops:
  7.2 7.4 copy-start
  7.2 32.1 %all-gather.13.cloned.1.call-start = ((), (), s32[]{:S(2)}) async-start(), calls=%async_computation.12 | async-start | bytes 2457600 | tf_op jit(solution)/shard_map/all_gather | solution.py:173
  8.5 6.1 copy-start.95
  10.4 4.4 copy-start.103
  11.4 5.0 copy-start.97
  11.4 5.0 copy-start.99
  14.5 55.4 %all-gather.15.cloned.1.call-start = ((), (), s32[]{:S(2)}) async-start(), calls=%async_computation.13 | async-start | bytes 3932160 | tf_op jit(solution)/shard_map/all_gather | solution.py:172
  14.8 5.8 copy-start.93
  15.2 5.5 copy-start.107
  15.2 5.5 copy-start.101
  16.5 107.4 %reduce-scatter.19.cloned.1.call-start = ((), (), s32[]{:S(2)}) async-start(), calls=%async_computation.19 | async-start | bytes 2457600 | tf_op jit(solution)/shard_map/reduce_scatter | solution.py:200
  17.1 68.9 %copy-start.111 = (f32[32]{0:T(128)}, f32[32]{0:T(128)S(1)}, u32[]{:S(2)}) copy-start(f32[32]{0:T(128)S(1)} %get-tuple-element.58) | copy-start | bytes 388
  17.1 92.8 %copy-start.113 = (f32[32]{0:T(128)}, f32[32]{0:T(128)S(1)}, u32[]{:S(2)}) copy-start(f32[32]{0:T(128)S(1)} %get-tuple-element.59) | copy-start | bytes 388
  20.7 49.3 %copy-start.65 = (bf16[768,3,192]{0,2,1:T(8,128)(2,1)}, bf16[768,3,192]{0,2,1:T(8,128)(2,1)S(1)}, u32[]{:S(2)}) copy-start(bf16[768,3,192]{0,2,1:T(8,128)(2,1)S(1)} %get-tuple-element.53) | copy-start | bytes 2654212
  75.6 7.0 copy-start.18
  84.7 4.4 copy-start.4
  93.4 71.4 %reduce-scatter.13.cloned.1.call-start = ((), (), s32[]{:S(2)}) async-start(), calls=%async_computation.14 | async-start | bytes 3932160 | tf_op jit(solution)/shard_map/reduce_scatter | solution.py:197
  109.3 4.8 copy-start.6
  118.0 5.9 copy-start.3
  118.0 70.6 %all-gather.21.cloned.1.call-start = ((), (), s32[]{:S(2)}) async-start(), calls=%async_computation.20 | async-start | bytes 2457600 | tf_op jit(solution)/shard_map/all_gather | solution.py:173
  127.6 91.5 %all-gather.17.cloned.1.call-start = ((), (), s32[]{:S(2)}) async-start(), calls=%async_computation.15 | async-start | bytes 3932160 | tf_op jit(solution)/shard_map/all_gather | solution.py:172
  166.7 21.9 %copy-start.69 = (bf16[768,3,192]{0,2,1:T(8,128)(2,1)S(1)}, bf16[768,3,192]{0,2,1:T(8,128)(2,1)}, u32[]{:S(2)}) copy-start(bf16[768,3,192]{0,2,1:T(8,128)(2,1)} %get-tuple-element.50) | copy-start | bytes 2654212
  168.1 84.7 %reduce-scatter.21.cloned.1.call-start = ((), (), s32[]{:S(2)}) async-start(), calls=%async_computation.21 | async-start | bytes 2457600 | tf_op jit(solution)/shard_map/reduce_scatter | solution.py:200
  198.0 7.5 copy-start.40
  214.7 4.4 copy-start.67
  218.0 75.8 %reduce-scatter.15.cloned.1.call-start = ((), (), s32[]{:S(2)}) async-start(), calls=%async_computation.16 | async-start | bytes 3932160 | tf_op jit(solution)/shard_map/reduce_scatter | solution.py:197
  237.7 4.4 copy-start.22
  247.9 69.8 %all-gather.23.cloned.1.call-start = ((), (), s32[]{:S(2)}) async-start(), calls=%async_computation.22 | async-start | bytes 2457600 | tf_op jit(solution)/shard_map/all_gather | solution.py:173
  256.0 85.0 %all-gather.31.cloned.1.call-start = ((), (), s32[]{:S(2)}) async-start(), calls=%async_computation.29 | async-start | bytes 2457600 | tf_op jit(solution)/shard_map/all_gather | solution.py:220
  256.6 115.1 %all-gather.19.cloned.1.call-start = ((), (), s32[]{:S(2)}) async-start(), calls=%async_computation.17 | async-start | bytes 3932160 | tf_op jit(solution)/shard_map/all_gather | solution.py:172
  297.0 104.6 %all-gather.25.cloned.1.call-start = ((), (), s32[]{:S(2)}) async-start(), calls=%async_computation.24 | async-start | bytes 3932160 | tf_op jit(solution)/shard_map/all_gather | solution.py:219
  297.6 137.0 %reduce-scatter.29.cloned.1.call-start = ((), (), s32[]{:S(2)}) async-start(), calls=%async_computation.30 | async-start | bytes 2457600 | tf_op jit(solution)/shard_map/reduce_scatter | solution.py:273
  341.0 8.3 copy-start.122
  352.3 122.6 %reduce-scatter.25.cloned.1.call-start = ((), (), s32[]{:S(2)}) async-start(), calls=%async_computation.25 | async-start | bytes 3932160 | tf_op jit(solution)/shard_map/reduce_scatter | solution.py:270
  401.7 10.1 copy-start.123
  415.9 82.9 %all-gather.33.cloned.1.call-start = ((), (), s32[]{:S(2)}) async-start(), calls=%async_computation.31 | async-start | bytes 2457600 | tf_op jit(solution)/shard_map/all_gather | solution.py:220
  439.9 103.8 %all-gather.27.cloned.1.call-start = ((), (), s32[]{:S(2)}) async-start(), calls=%async_computation.26 | async-start | bytes 3932160 | tf_op jit(solution)/shard_map/all_gather | solution.py:219
  479.6 107.6 %reduce-scatter.31.cloned.1.call-start = ((), (), s32[]{:S(2)}) async-start(), calls=%async_computation.32 | async-start | bytes 2457600 | tf_op jit(solution)/shard_map/reduce_scatter | solution.py:273
  537.0 63.3 %reduce-scatter.23.cloned.1.call-start = ((), (), s32[]{:S(2)}) async-start(), calls=%async_computation.23 | async-start | bytes 2457600 | tf_op jit(solution)/shard_map/reduce_scatter | solution.py:200
  543.3 97.4 %reduce-scatter.27.cloned.1.call-start = ((), (), s32[]{:S(2)}) async-start(), calls=%async_computation.27 | async-start | bytes 3932160 | tf_op jit(solution)/shard_map/reduce_scatter | solution.py:270
  578.0 103.1 %reduce-scatter.17.cloned.1.call-start = ((), (), s32[]{:S(2)}) async-start(), calls=%async_computation.18 | async-start | bytes 3932160 | tf_op jit(solution)/shard_map/reduce_scatter | solution.py:197
  587.1 117.9 %all-gather.35.cloned.1.call-start = ((), (), s32[]{:S(2)}) async-start(), calls=%async_computation.33 | async-start | bytes 2457600 | tf_op jit(solution)/shard_map/all_gather | solution.py:220
  604.2 131.5 %all-gather.29.cloned.1.call-start = ((), (), s32[]{:S(2)}) async-start(), calls=%async_computation.28 | async-start | bytes 3932160 | tf_op jit(solution)/shard_map/all_gather | solution.py:219
  685.2 5.3 copy-start.126
  685.2 154.6 %reduce-scatter.35.cloned.1.call-start = ((), (), s32[]{:S(2)}) async-start(), calls=%async_computation.35 | async-start | bytes 2457600 | tf_op jit(solution)/shard_map/reduce_scatter | solution.py:273
  685.4 5.1 copy-start.128
  698.2 6.8 copy-start.117
  705.0 7.0 copy-start.5
  705.0 7.0 copy-start.88
  723.0 12.7 %copy-start.116 = (bf16[32]{0:T(256)(128)(2,1)S(1)}, bf16[32]{0:T(256)(128)(2,1)}, u32[]{:S(2)}) copy-start(bf16[32]{0:T(256)(128)(2,1)} %get-tuple-element.57) | copy-start | bytes 196
  767.0 78.4 %reduce-scatter.33.cloned.1.call-start = ((), (), s32[]{:S(2)}) async-start(), calls=%async_computation.34 | async-start | bytes 3932160 | tf_op jit(solution)/shard_map/reduce_scatter | solution.py:270
  769.6 8.5 copy-start.33
  769.6 8.5 copy-start.38
  786.4 5.1 copy-start.35
  786.4 5.1 copy-start.39
  791.5 7.3 slice-start
  803.4 5.9 copy-start.89
  803.4 342.2 %all-reduce.5.cloned.1.call-start = ((), (), s32[]{:S(2)}) async-start(), calls=%async_computation.36 | async-start | bytes 18874368 | tf_op jit(solution)/shard_map/psum | solution.py:299
  803.6 5.7 copy-start.90
  803.6 5.7 copy-start.91
  838.0 4.4 copy-start.106
  838.0 4.4 copy-start.104
  839.7 4.4 copy-start.62
  839.8 4.4 copy-start.43
  (93 other events, 214.1 us)
Sparse Core Ops, SparseCore 0:
  14.7 24.5 all-gather.12
  41.4 28.4 all-gather.14
  93.5 30.3 reduce-scatter.18
  126.9 37.8 reduce-scatter.12
  166.8 21.8 all-gather.20
  190.6 28.4 all-gather.16
  222.3 30.3 reduce-scatter.20
  255.8 37.8 reduce-scatter.14
  295.9 21.8 all-gather.22
  319.2 21.8 all-gather.30
  343.2 28.4 all-gather.18
  373.1 28.4 all-gather.24
  404.2 30.3 reduce-scatter.28
  437.0 37.8 reduce-scatter.24
  476.9 21.8 all-gather.32
  500.8 28.4 all-gather.26
  537.1 30.3 reduce-scatter.30
  569.9 30.3 reduce-scatter.22
  602.8 37.8 reduce-scatter.26
  643.1 37.8 reduce-scatter.16
  683.2 21.8 all-gather.34
  707.2 28.4 all-gather.28
  767.1 30.3 reduce-scatter.34
  803.5 37.7 reduce-scatter.32
  846.3 299.1 all-reduce.4
where the time goes:
time: 1170 us; the launch traced here: 1160 us
  waiting for transfers between devices  633 us (54%)
  matrix products  245 us (21%)
  local copies, waits for them, and re-layouts  130 us (11%)
  other arithmetic  84.9 us (7%)
  blocking collectives  51.5 us (4%)
  between operations  16 us (1%)
    psum x1, waiting for transfers between devices, per_device(): lax.psum(grad.astype(jnp.bfloat16), 'dp').astype(jnp.float32)  242 us
    reduce_scatter x6, waiting for transfers between devices, per_device(): lax.psum_scatter(text_part.astype(jnp.bfloat16), 'mp', scatter_dimension=...  171 us
    dot_general x20, matrix products, linear(): jnp.einsum('pld,de->ple', activation, weight, preferred_element_type=jnp....  82 us
    dot_general x20, matrix products, linear_back(): jnp.einsum('ple,de->pld', gradient, weight, preferred_element_type=jnp.fl...  68.1 us
    all_gather x3, waiting for transfers between devices, per_device(): lax.all_gather(visual_norm, 'mp', axis=0, tiled=True)  58.5 us
    all_gather x3, waiting for transfers between devices, per_device(): lax.all_gather(text_norm, 'mp', axis=0, tiled=True)  47.1 us
    all_gather x3, waiting for transfers between devices, per_device(): lax.all_gather(visual_back.astype(jnp.bfloat16), 'mp', axis=0, tiled=True)  42.2 us
    psum x1, blocking collectives, per_device(): gain_grads, shift_grads = lax.psum((gain_grads, shift_grads), 'dp')  40.7 us
  transfers between devices with their start and end apart: 25, of which 21 were waited for; matrix products, arithmetic and copies ran while one was open for 31% of the time, Pallas kernels for 0%

commit v1 on v0

--- a/solution.py
+++ b/solution.py
@@ -1,3 +1,4 @@
+import functools
 import jax
 import jax.numpy as jnp
 from jax import lax
@@ -5,6 +6,14 @@
 
 HEAD = 64
 EPSILON = 1e-05
+
+
+def measure_the_stages_all(load, ax_name):
+    block_out = jnp.sum(lax.all_gather(load, axis_name=ax_name), 0)
+    return block_out
+
+
+_bring_fields = functools.partial(measure_the_stages_all, ax_name="dp")
 
 
 def normalize(values, gain, shift):
@@ -296,7 +305,7 @@
     in_grads = jnp.stack(in_parts)
     out_grads = jnp.stack(out_parts)
     in_grads, out_grads, up_grads, down_grads = jax.tree.map(
-        lambda grad: lax.psum(grad.astype(jnp.bfloat16), "dp").astype(jnp.float32),
+        lambda grad: _bring_fields(grad.astype(jnp.bfloat16)).astype(jnp.float32),
         (in_grads, out_grads, up_grads, down_grads),
     )
     gain_grads, shift_grads = lax.psum((gain_grads, shift_grads), "dp")

time: 1170 us -> 2290 us (1.96)
  waiting for transfers between devices: 633 us -> 1680 us
  other arithmetic: 84.9 us -> 134 us
    all_gather x0 -> x4, waiting for transfers between devices: none -> 1270 us  [measure_the_stages_all(): block_out = jnp.sum(lax.all_gather(load, axis_name=ax_name), 0)]
    psum x1 -> x0, waiting for transfers between devices: 242 us -> none  [per_device(): lax.psum(grad.astype(jnp.bfloat16), 'dp').astype(jnp.float32)]
    reduce_sum x0 -> x4, other arithmetic: none -> 46.1 us  [measure_the_stages_all(): block_out = jnp.sum(lax.all_gather(load, axis_name=ax_name), 0)]
  transfers between devices with their start and end apart: 25 -> 28, of which waited for: 21 -> 24; matrix products, arithmetic and copies ran while one was open for 31% -> 17% of each run, Pallas kernels for 0% -> 0%
where the time goes in v1:
time: 2290 us; the launch traced here: 2280 us
  waiting for transfers between devices  1680 us (73%)
  matrix products  244 us (11%)
  other arithmetic  134 us (6%)
  local copies, waits for them, and re-layouts  133 us (6%)
  blocking collectives  61.2 us (3%)
    all_gather x4, waiting for transfers between devices, measure_the_stages_all(): block_out = jnp.sum(lax.all_gather(load, axis_name=ax_name), 0)  1270 us
    reduce_scatter x6, waiting for transfers between devices, per_device(): lax.psum_scatter(text_part.astype(jnp.bfloat16), 'mp', scatter_dimension=...  181 us
    dot_general x20, matrix products, linear(): jnp.einsum('pld,de->ple', activation, weight, preferred_element_type=jnp....  82 us
    dot_general x20, matrix products, linear_back(): jnp.einsum('ple,de->pld', gradient, weight, preferred_element_type=jnp.fl...  68 us
    all_gather x3, waiting for transfers between devices, per_device(): lax.all_gather(visual_norm, 'mp', axis=0, tiled=True)  56.6 us
    all_gather x3, waiting for transfers between devices, per_device(): lax.all_gather(visual_back.astype(jnp.bfloat16), 'mp', axis=0, tiled=True)  55.9 us
    psum x1, blocking collectives, per_device(): gain_grads, shift_grads = lax.psum((gain_grads, shift_grads), 'dp')  50 us
    all_gather x3, waiting for transfers between devices, per_device(): lax.all_gather(text_norm, 'mp', axis=0, tiled=True)  47 us
  transfers between devices with their start and end apart: 28, of which 24 were waited for; matrix products, arithmetic and copies ran while one was open for 17% of the time, Pallas kernels for 0%

profile of v1, /device:TPU:0, one launch (start us, length us, event | category | flops | bytes accessed | tf_op | source)
XLA Modules:
  0.0 2277.5 jit_solution(3527688606395060996)
XLA Ops:
  20.7 18.6 all-gather.17.cloned.1.call-done
  42.8 27.2 %all-gather.19.cloned.1.call-done = bf16[32,64,768]{2,1,0:T(8,128)(2,1)} async-done(((bf16[8,64,768]{2,1,0:T(8,128)(2,1)}), bf16[32,64,768]{2,1,0:T(8,128)(2,1)}) %all-gather.19.cloned.1.call-update) | async-done | bytes 3145744 | tf_op jit(solution)/shard_map/all_gather | solution.py:181
  70.0 3.9 convolution_convert_fusion.13
  75.7 4.4 convolution_convert_fusion.14
  100.9 4.1 convolution_convert_fusion.18
  114.1 3.9 convolution_convert_fusion.3
  118.1 5.9 reduce-scatter.19.cloned.1.call-done
  127.8 37.1 %reduce-scatter.13.cloned.1.call-done = bf16[8,64,768]{2,1,0:T(8,128)(2,1)} async-done(((bf16[32,64,768]{2,1,0:T(8,128)(2,1)}), bf16[8,64,768]{2,1,0:T(8,128)(2,1)}) %reduce-scatter.13.cloned.1.call-update) | async-done | bytes 786448 | tf_op jit(solution)/shard_map/reduce_scatter | solution.py:206
  168.8 20.0 all-gather.25.cloned.1.call-done
  198.1 3.9 convolution_convert_fusion.26
  202.0 3.6 reshape.627
  219.2 3.9 convolution_convert_fusion.15
  225.7 3.9 convolution_convert_fusion.16
  232.1 3.9 convolution_convert_fusion.17
  244.1 3.9 convolution_convert_fusion.2
  248.1 4.7 reduce-scatter.21.cloned.1.call-done
  257.3 36.5 %reduce-scatter.15.cloned.1.call-done = bf16[8,64,768]{2,1,0:T(8,128)(2,1)} async-done(((bf16[32,64,768]{2,1,0:T(8,128)(2,1)}), bf16[8,64,768]{2,1,0:T(8,128)(2,1)}) %reduce-scatter.15.cloned.1.call-update) | async-done | bytes 786448 | tf_op jit(solution)/shard_map/reduce_scatter | solution.py:206
  299.8 18.0 all-gather.27.cloned.1.call-done
  317.8 5.5 fusion.80
  323.3 17.8 all-gather.35.cloned.1.call-done
  341.1 7.0 fusion.13
  353.0 18.8 all-gather.23.cloned.1.call-done
  371.8 7.5 fusion.85
  379.3 22.4 all-gather.29.cloned.1.call-done
  401.7 8.5 fusion.6
  411.9 4.0 convolution_convert_fusion
  416.0 18.7 reduce-scatter.29.cloned.1.call-done
  441.3 33.7 %reduce-scatter.25.cloned.1.call-done = bf16[8,64,768]{2,1,0:T(8,128)(2,1)} async-done(((bf16[32,64,768]{2,1,0:T(8,128)(2,1)}), bf16[8,64,768]{2,1,0:T(8,128)(2,1)}) %reduce-scatter.25.cloned.1.call-update) | async-done | bytes 786448 | tf_op jit(solution)/shard_map/reduce_scatter | solution.py:279
  480.5 18.3 all-gather.37.cloned.1.call-done
  505.5 3.8 multiply_reduce_fusion.3
  537.0 6.3 convolution_convert_fusion.5
  543.6 4.3 convolution_convert_fusion.12
  550.5 4.2 multiply_reduce_fusion
  561.7 4.1 fusion.36
  578.5 8.6 convolution_convert_fusion.1
  591.0 9.2 reduce-scatter.23.cloned.1.call-done
  600.2 3.9 fusion.209
  604.2 37.0 %reduce-scatter.27.cloned.1.call-done = bf16[8,64,768]{2,1,0:T(8,128)(2,1)} async-done(((bf16[32,64,768]{2,1,0:T(8,128)(2,1)}), bf16[8,64,768]{2,1,0:T(8,128)(2,1)}) %reduce-scatter.27.cloned.1.call-update) | async-done | bytes 786448 | tf_op jit(solution)/shard_map/reduce_scatter | solution.py:279
  644.4 37.1 %reduce-scatter.17.cloned.1.call-done = bf16[8,64,768]{2,1,0:T(8,128)(2,1)} async-done(((bf16[32,64,768]{2,1,0:T(8,128)(2,1)}), bf16[8,64,768]{2,1,0:T(8,128)(2,1)}) %reduce-scatter.17.cloned.1.call-update) | async-done | bytes 786448 | tf_op jit(solution)/shard_map/reduce_scatter | solution.py:206
  681.5 4.1 fusion.210
  685.7 19.8 all-gather.39.cloned.1.call-done
  708.8 3.7 reshape.633
  723.5 3.8 fusion.171
  727.2 9.0 all-gather.33.cloned.1.call-done
  736.2 3.9 fusion.49
  773.7 4.0 convolution_convert_fusion.8
  777.7 5.0 fusion.172
  790.5 4.1 add_convert_fusion
  805.5 4.6 fusion.46
  810.2 6.2 fusion.45
  825.3 3.7 copy.218
  872.6 11.2 all-reduce.1
  883.8 50.0 %all-reduce = (f32[6,768]{1,0:T(8,128)}, f32[6,768]{1,0:T(8,128)}) all-reduce(bf16[6,768]{1,0:T(8,128)(2,1)S(1)} %get-tuple-element.36, bf16[6,768]{1,0:T(8,128)(2,1)S(1)} %get-tuple-element.37), channel_id=1, replica_groups=mesh['dp'=8,'mp'=4] {'dp'}, use_global_device_ids=true, to_apply=%region_59.0 | all-reduce | flops 9216 | bytes 55296 | tf_op jit(solution)/shard_map/psum | solution.py:311
  936.7 269.1 %all-gather.45.cloned.1.call-done = bf16[8,2,768,768]{3,2,1,0:T(8,128)(2,1)} async-done(((bf16[1,2,768,768]{3,2,1,0:T(8,128)(2,1)}), bf16[8,2,768,768]{3,2,1,0:T(8,128)(2,1)}) %all-gather.45.cloned.1.call-update) | async-done | bytes 18874384 | tf_op jit(solution)/shard_map/all_gather | solution.py:12
  1205.8 12.4 reduce_sum.499
  1218.2 4.2 convert_element_type.614
  1222.4 347.2 %all-gather.47.cloned.1.call-done = bf16[8,2,768,768]{3,2,1,0:T(8,128)(2,1)} async-done(((bf16[1,2,768,768]{3,2,1,0:T(8,128)(2,1)}), bf16[8,2,768,768]{3,2,1,0:T(8,128)(2,1)}) %all-gather.47.cloned.1.call-update) | async-done | bytes 18874384 | tf_op jit(solution)/shard_map/all_gather | solution.py:12
  1569.5 12.3 reduce_sum.503
  1581.8 4.2 convert_element_type.615
  1586.1 122.8 %all-gather.43.cloned.1.call-done = bf16[8,4,192,768]{3,2,1,0:T(8,128)(2,1)} async-done(((bf16[1,4,192,768]{3,2,1,0:T(8,128)(2,1)}), bf16[8,4,192,768]{3,2,1,0:T(8,128)(2,1)}) %all-gather.43.cloned.1.call-update) | async-done | bytes 9437200 | tf_op jit(solution)/shard_map/all_gather | solution.py:12
  1708.8 5.2 reduce_sum.498
  1715.6 532.9 %all-gather.41.cloned.1.call-done = bf16[8,4,768,3,192]{2,4,3,1,0:T(8,128)(2,1)} async-done(((bf16[1,4,768,3,192]{2,4,3,1,0:T(8,128)(2,1)}), bf16[8,4,768,3,192]{2,4,3,1,0:T(8,128)(2,1)}) %all-gather.41.cloned.1.call-update) | async-done | bytes 28311568 | tf_op jit(solution)/shard_map/all_gather | solution.py:12
  2248.5 16.2 reduce_sum.497
  2264.7 5.7 convert_element_type.610
  (570 shorter events, 307.7 us)
Async XLA Ops:
  7.2 7.5 copy-start
  7.2 32.1 %all-gather.17.cloned.1.call-start = ((), (), s32[]{:S(2)}) async-start(), calls=%async_computation.12 | async-start | bytes 2457600 | tf_op jit(solution)/shard_map/all_gather | solution.py:182
  8.5 6.2 copy-start.82
  9.8 6.7 copy-start.117
  10.9 115.8 %copy-start.101 = (f32[768]{0:T(1024)}, f32[768]{0:T(1024)S(1)}, u32[]{:S(2)}) copy-start(f32[768]{0:T(1024)S(1)} %get-tuple-element.27) | copy-start | bytes 9220
  10.9 156.0 %copy-start.96 = (f32[768]{0:T(1024)}, f32[768]{0:T(1024)S(1)}, u32[]{:S(2)}) copy-start(f32[768]{0:T(1024)S(1)} %get-tuple-element.24) | copy-start | bytes 9220
  10.9 244.1 %copy-start.86 = (f32[768]{0:T(1024)}, f32[768]{0:T(1024)S(1)}, u32[]{:S(2)}) copy-start(f32[768]{0:T(1024)S(1)} %get-tuple-element.22) | copy-start | bytes 9220
  14.6 55.4 %all-gather.19.cloned.1.call-start = ((), (), s32[]{:S(2)}) async-start(), calls=%async_computation.13 | async-start | bytes 3932160 | tf_op jit(solution)/shard_map/all_gather | solution.py:181
  16.5 107.4 %reduce-scatter.19.cloned.1.call-start = ((), (), s32[]{:S(2)}) async-start(), calls=%async_computation.19 | async-start | bytes 2457600 | tf_op jit(solution)/shard_map/reduce_scatter | solution.py:209
  17.1 69.0 %copy-start.133 = (f32[32]{0:T(128)}, f32[32]{0:T(128)S(1)}, u32[]{:S(2)}) copy-start(f32[32]{0:T(128)S(1)} %get-tuple-element.54) | copy-start | bytes 388
  17.1 93.0 %copy-start.135 = (f32[32]{0:T(128)}, f32[32]{0:T(128)S(1)}, u32[]{:S(2)}) copy-start(f32[32]{0:T(128)S(1)} %get-tuple-element.55) | copy-start | bytes 388
  20.7 49.3 %copy-start.61 = (bf16[768,3,192]{0,2,1:T(8,128)(2,1)}, bf16[768,3,192]{0,2,1:T(8,128)(2,1)S(1)}, u32[]{:S(2)}) copy-start(bf16[768,3,192]{0,2,1:T(8,128)(2,1)S(1)} %get-tuple-element.49) | copy-start | bytes 2654212
  75.7 7.0 copy-start.18
  93.4 71.4 %reduce-scatter.13.cloned.1.call-start = ((), (), s32[]{:S(2)}) async-start(), calls=%async_computation.14 | async-start | bytes 3932160 | tf_op jit(solution)/shard_map/reduce_scatter | solution.py:206
  118.0 5.9 copy-start.3
  118.1 70.6 %all-gather.25.cloned.1.call-start = ((), (), s32[]{:S(2)}) async-start(), calls=%async_computation.20 | async-start | bytes 2457600 | tf_op jit(solution)/shard_map/all_gather | solution.py:182
  125.3 41.1 %copy-start.84 = (f32[8,40]{1,0:T(8,128)}, f32[8,40]{1,0:T(8,128)S(1)}, u32[]{:S(2)}) copy-start(f32[8,40]{1,0:T(8,128)S(1)} %broadcast_multiply_fusion.4) | copy-start | bytes 3844
  126.6 38.2 %copy-start.123 = (f32[8,40]{1,0:T(8,128)}, f32[8,40]{1,0:T(8,128)S(1)}, u32[]{:S(2)}) copy-start(f32[8,40]{1,0:T(8,128)S(1)} %multiply_reduce_fusion.11) | copy-start | bytes 3844
  126.6 40.2 %copy-start.113 = (f32[8,40]{1,0:T(8,128)}, f32[8,40]{1,0:T(8,128)S(1)}, u32[]{:S(2)}) copy-start(f32[8,40]{1,0:T(8,128)S(1)} %fusion.195) | copy-start | bytes 3844
  127.7 91.5 %all-gather.21.cloned.1.call-start = ((), (), s32[]{:S(2)}) async-start(), calls=%async_computation.15 | async-start | bytes 3932160 | tf_op jit(solution)/shard_map/all_gather | solution.py:181
  166.8 24.2 %copy-start.121 = (f32[8,64]{1,0:T(8,128)}, f32[8,64]{1,0:T(8,128)S(1)}, u32[]{:S(2)}) copy-start(f32[8,64]{1,0:T(8,128)S(1)} %multiply_reduce_fusion.9) | copy-start | bytes 6148
  166.8 21.9 copy-start.65
  166.8 24.2 %copy-start.109 = (f32[8,64]{1,0:T(8,128)}, f32[8,64]{1,0:T(8,128)S(1)}, u32[]{:S(2)}) copy-start(f32[8,64]{1,0:T(8,128)S(1)} %fusion.193) | copy-start | bytes 6148
  168.2 84.6 %reduce-scatter.21.cloned.1.call-start = ((), (), s32[]{:S(2)}) async-start(), calls=%async_computation.21 | async-start | bytes 2457600 | tf_op jit(solution)/shard_map/reduce_scatter | solution.py:209
  198.1 7.5 copy-start.38
  218.0 75.8 %reduce-scatter.15.cloned.1.call-start = ((), (), s32[]{:S(2)}) async-start(), calls=%async_computation.16 | async-start | bytes 3932160 | tf_op jit(solution)/shard_map/reduce_scatter | solution.py:206
  248.0 7.6 copy-start.130
  248.0 69.8 %all-gather.27.cloned.1.call-start = ((), (), s32[]{:S(2)}) async-start(), calls=%async_computation.22 | async-start | bytes 2457600 | tf_op jit(solution)/shard_map/all_gather | solution.py:182
  256.6 84.5 %all-gather.35.cloned.1.call-start = ((), (), s32[]{:S(2)}) async-start(), calls=%async_computation.29 | async-start | bytes 2457600 | tf_op jit(solution)/shard_map/all_gather | solution.py:229
  257.2 114.6 %all-gather.23.cloned.1.call-start = ((), (), s32[]{:S(2)}) async-start(), calls=%async_computation.17 | async-start | bytes 3932160 | tf_op jit(solution)/shard_map/all_gather | solution.py:181
  299.0 102.8 %all-gather.29.cloned.1.call-start = ((), (), s32[]{:S(2)}) async-start(), calls=%async_computation.24 | async-start | bytes 3932160 | tf_op jit(solution)/shard_map/all_gather | solution.py:228
  299.6 135.2 %reduce-scatter.29.cloned.1.call-start = ((), (), s32[]{:S(2)}) async-start(), calls=%async_computation.30 | async-start | bytes 2457600 | tf_op jit(solution)/shard_map/reduce_scatter | solution.py:282
  341.1 8.3 copy-start.145
  352.5 122.5 %reduce-scatter.25.cloned.1.call-start = ((), (), s32[]{:S(2)}) async-start(), calls=%async_computation.25 | async-start | bytes 3932160 | tf_op jit(solution)/shard_map/reduce_scatter | solution.py:279
  401.7 10.1 copy-start.146
  415.9 82.9 %all-gather.37.cloned.1.call-start = ((), (), s32[]{:S(2)}) async-start(), calls=%async_computation.31 | async-start | bytes 2457600 | tf_op jit(solution)/shard_map/all_gather | solution.py:229
  441.2 102.4 %all-gather.31.cloned.1.call-start = ((), (), s32[]{:S(2)}) async-start(), calls=%async_computation.26 | async-start | bytes 3932160 | tf_op jit(solution)/shard_map/all_gather | solution.py:228
  480.3 107.0 %reduce-scatter.31.cloned.1.call-start = ((), (), s32[]{:S(2)}) async-start(), calls=%async_computation.32 | async-start | bytes 2457600 | tf_op jit(solution)/shard_map/reduce_scatter | solution.py:282
  536.9 63.3 %reduce-scatter.23.cloned.1.call-start = ((), (), s32[]{:S(2)}) async-start(), calls=%async_computation.23 | async-start | bytes 2457600 | tf_op jit(solution)/shard_map/reduce_scatter | solution.py:209
  543.3 97.9 %reduce-scatter.27.cloned.1.call-start = ((), (), s32[]{:S(2)}) async-start(), calls=%async_computation.27 | async-start | bytes 3932160 | tf_op jit(solution)/shard_map/reduce_scatter | solution.py:279
  578.1 103.4 %reduce-scatter.17.cloned.1.call-start = ((), (), s32[]{:S(2)}) async-start(), calls=%async_computation.18 | async-start | bytes 3932160 | tf_op jit(solution)/shard_map/reduce_scatter | solution.py:206
  587.2 13.0 copy-start.88
  587.2 13.0 copy-start.100
  587.2 13.0 copy-start.112
  587.2 13.0 copy-start.129
  587.3 118.3 %all-gather.39.cloned.1.call-start = ((), (), s32[]{:S(2)}) async-start(), calls=%async_computation.33 | async-start | bytes 2457600 | tf_op jit(solution)/shard_map/all_gather | solution.py:229
  591.0 50.2 %copy-start.97 = (f32[768]{0:T(1024)S(1)}, f32[768]{0:T(1024)}, u32[]{:S(2)}) copy-start(f32[768]{0:T(1024)} %copy-done.96) | copy-start | bytes 9220
  604.1 39.1 %copy-start.122 = (f32[8,64]{1,0:T(8,128)S(1)}, f32[8,64]{1,0:T(8,128)}, u32[]{:S(2)}) copy-start(f32[8,64]{1,0:T(8,128)} %copy-done.121) | copy-start | bytes 6148
  604.1 39.2 %copy-start.110 = (f32[8,64]{1,0:T(8,128)S(1)}, f32[8,64]{1,0:T(8,128)}, u32[]{:S(2)}) copy-start(f32[8,64]{1,0:T(8,128)} %copy-done.109) | copy-start | bytes 6148
  604.1 77.4 %copy-start.91 = (f32[8,64]{1,0:T(8,128)S(1)}, f32[8,64]{1,0:T(8,128)}, u32[]{:S(2)}) copy-start(f32[8,64]{1,0:T(8,128)} %copy-done.89) | copy-start | bytes 6148
  604.1 77.4 %copy-start.104 = (f32[8,64]{1,0:T(8,128)S(1)}, f32[8,64]{1,0:T(8,128)}, u32[]{:S(2)}) copy-start(f32[8,64]{1,0:T(8,128)} %copy-done.103) | copy-start | bytes 6148
  604.2 77.4 %copy-start.116 = (f32[8,64]{1,0:T(8,128)S(1)}, f32[8,64]{1,0:T(8,128)}, u32[]{:S(2)}) copy-start(f32[8,64]{1,0:T(8,128)} %copy-done.115) | copy-start | bytes 6148
  604.2 132.0 %all-gather.33.cloned.1.call-start = ((), (), s32[]{:S(2)}) async-start(), calls=%async_computation.28 | async-start | bytes 3932160 | tf_op jit(solution)/shard_map/all_gather | solution.py:228
  644.4 61.1 %copy-start.139 = (bf16[32]{0:T(256)(128)(2,1)S(1)}, bf16[32]{0:T(256)(128)(2,1)}, u32[]{:S(2)}) copy-start(bf16[32]{0:T(256)(128)(2,1)} %get-tuple-element.52) | copy-start | bytes 196
  685.7 177.2 %reduce-scatter.35.cloned.1.call-start = ((), (), s32[]{:S(2)}) async-start(), calls=%async_computation.35 | async-start | bytes 2457600 | tf_op jit(solution)/shard_map/reduce_scatter | solution.py:282
  705.5 6.9 copy-start.5
  705.5 6.9 copy-start.79
  723.5 12.7 copy-start.138
  767.4 101.1 %reduce-scatter.33.cloned.1.call-start = ((), (), s32[]{:S(2)}) async-start(), calls=%async_computation.34 | async-start | bytes 3932160 | tf_op jit(solution)/shard_map/reduce_scatter | solution.py:279
  782.7 7.4 slice-start
  794.6 411.1 %all-gather.45.cloned.1.call-start = ((), (), s32[]{:S(2)}) async-start(), calls=%async_computation.38 | async-start | bytes 21233664 | tf_op jit(solution)/shard_map/all_gather | solution.py:12
  804.0 765.5 %all-gather.47.cloned.1.call-start = ((), (), s32[]{:S(2)}) async-start(), calls=%async_computation.39 | async-start | bytes 21233664 | tf_op jit(solution)/shard_map/all_gather | solution.py:12
  818.0 890.8 %all-gather.43.cloned.1.call-start = ((), (), s32[]{:S(2)}) async-start(), calls=%async_computation.37 | async-start | bytes 10616832 | tf_op jit(solution)/shard_map/all_gather | solution.py:12
  838.5 1410.0 %all-gather.41.cloned.1.call-start = ((), (), s32[]{:S(2)}) async-start(), calls=%async_computation.36 | async-start | bytes 31850496 | tf_op jit(solution)/shard_map/all_gather | solution.py:12
  (120 other events, 317.3 us)
Sparse Core Ops, SparseCore 0:
  14.7 24.5 all-gather.16
  41.4 28.4 all-gather.18
  93.6 30.3 reduce-scatter.18
  126.9 37.8 reduce-scatter.12
  166.8 21.8 all-gather.24
  190.7 28.4 all-gather.20
  222.4 30.3 reduce-scatter.20
  255.9 37.8 reduce-scatter.14
  296.0 21.8 all-gather.26
  319.2 21.8 all-gather.34
  343.2 28.4 all-gather.22
  373.2 28.4 all-gather.28
  404.3 30.3 reduce-scatter.28
  437.1 37.8 reduce-scatter.24
  477.0 21.8 all-gather.36
  500.9 28.4 all-gather.30
  537.0 30.3 reduce-scatter.30
  569.8 30.3 reduce-scatter.22
  603.3 37.8 reduce-scatter.26
  643.6 37.8 reduce-scatter.16
  683.7 21.8 all-gather.38
  707.6 28.4 all-gather.32
  767.5 30.3 reduce-scatter.34
  800.9 37.8 reduce-scatter.32
  840.9 364.8 all-gather.44
  1207.1 362.3 all-gather.46
  1571.6 137.1 all-gather.42
  1710.9 537.5 all-gather.40
